TPU v7x, 32 devices: a whole 2x2x4 slice. The times are simulated.
32 devices in a mesh: box: 4 (over y, x), dir: 8 (over z, core).
Axes of the slice: x: 2, y: 2, z: 4, core: 2. Of those that a mesh axis runs over, the one named last changes fastest.
Arguments:
- currents: bfloat16 [2048, 512], P(('box', 'dir')), may hold values from -6 to 6
- near_list: int32 [2048, 27], P(('box', 'dir')), may hold values from 0 to 2047, as said below
- far_list: int32 [256, 20], replicated, may hold values from 0 to 255, as said below
- far_kind: int32 [256, 20], replicated, may hold values from 0 to 315
- aggregate: bfloat16 [512, 1024], replicated, may hold values from -0.25 to 0.25
- interp: bfloat16 [1024, 4096], replicated, may hold values from -0.1875 to 0.1875
- receive: bfloat16 [1024, 512], replicated, may hold values from -0.1875 to 0.1875
- shift_angle: float32 [8, 2048], replicated, may hold values from -3.140625 to 3.140625
- translation: float32 [316, 2, 2048], P(None, None, 'dir'), may hold values from -0.6 to 0.6
- near_matrix: bfloat16 [27, 512, 512], replicated, may hold values from -0.0546875 to 0.0546875
Outputs:
- fields: float32 [2048, 512], P(('box', 'dir'))
Inputs may be any that keep to these rules, and one draw needn't show every extreme that they name: `near_list`: entry [l, n] lies within 32 of l. `far_list`: entry [p, j] differs from p by 2 to 32.
All inputs are finite; a program needn't handle non-finite values.
Results may differ from a plain program's by a relative error of at most 0.013.
Values may be sent and summed in bfloat16 or wider, within the bound.
A program may use at most 128 MiB of HBM per device.

v0:
```python
import jax
import jax.numpy as jnp
from jax import lax
from jax.sharding import PartitionSpec as P


def padded_2(block, sides, width):
    for axis, dim in sides:
        count = lax.axis_size(axis)
        forward = [(i, i + 1) for i in range(count - 1)]
        backward = [(target, source) for source, target in forward]
        low = lax.ppermute(
            lax.slice_in_dim(block, block.shape[dim] - width, None, axis=dim), axis, forward
        )
        high = lax.ppermute(lax.slice_in_dim(block, 0, width, axis=dim), axis, backward)
        block = jnp.concatenate([low, block, high], axis=dim)
    return block


def translate(source_field, row_index, inside, kind_rows, translation):
    rows = row_index.shape[0]
    width = source_field.shape[2]
    real_acc = jnp.zeros((rows, width), jnp.float32)
    imag_acc = jnp.zeros((rows, width), jnp.float32)
    for slot in range(row_index.shape[1]):
        source = jnp.where(inside[:, slot, None, None], source_field[row_index[:, slot]], 0.0)
        operator = translation[kind_rows[:, slot]]
        real_acc = real_acc + operator[:, 0] * source[:, 0] - operator[:, 1] * source[:, 1]
        imag_acc = imag_acc + operator[:, 0] * source[:, 1] + operator[:, 1] * source[:, 0]
    return jnp.stack([real_acc, imag_acc], axis=1)


def on_device(
    currents,
    near_list,
    far_list,
    far_kind,
    aggregate,
    interp,
    receive,
    shift_angle,
    translation,
    near_matrix,
):
    leaf_dev = currents.shape[0]
    directions = shift_angle.shape[1]
    pattern = jnp.dot(currents, aggregate, preferred_element_type=jnp.float32).astype(jnp.bfloat16)
    children = jnp.dot(pattern, interp, preferred_element_type=jnp.float32).reshape(
        leaf_dev // 8, 8, 2, directions
    )
    cosine = jnp.cos(shift_angle)
    sine_part = jnp.sin(shift_angle)
    real_part = jnp.sum(children[:, :, 0] * cosine - children[:, :, 1] * sine_part, axis=1)
    imag_part = jnp.sum(children[:, :, 0] * sine_part + children[:, :, 1] * cosine, axis=1)
    parent = jnp.stack([real_part, imag_part], axis=1)
    upper = lax.all_to_all(
        parent.astype(jnp.bfloat16), "dir", split_axis=2, concat_axis=0, tiled=True
    ).astype(parent.dtype)
    upper_rows = upper.shape[0]
    far_reach = upper_rows // 2
    first_row = lax.axis_index("box") * upper_rows
    my_far = lax.dynamic_slice_in_dim(far_list, first_row, upper_rows, 0)
    my_kind = lax.dynamic_slice_in_dim(far_kind, first_row, upper_rows, 0)
    extended = padded_2(upper.astype(jnp.bfloat16), (("box", 0),), far_reach).astype(upper.dtype)
    local_index = my_far - (first_row - far_reach)
    inside = jnp.ones(my_far.shape, jnp.bool_)
    local_field = translate(extended, local_index, inside, my_kind, translation)
    incoming = lax.all_to_all(
        local_field.astype(jnp.bfloat16), "dir", split_axis=0, concat_axis=2, tiled=True
    ).astype(local_field.dtype)
    rot_real = incoming[:, None, 0] * cosine + incoming[:, None, 1] * sine_part
    rot_imag = incoming[:, None, 1] * cosine - incoming[:, None, 0] * sine_part
    received = (
        jnp.stack([rot_real, rot_imag], axis=2)
        .reshape(leaf_dev, 2 * directions)
        .astype(jnp.bfloat16)
    )
    back_pattern = lax.dot_general(
        received, interp, (((1,), (1,)), ((), ())), preferred_element_type=jnp.float32
    ).astype(jnp.bfloat16)
    fields = jnp.dot(back_pattern, receive, preferred_element_type=jnp.float32)
    near_reach = leaf_dev // 2
    padded = padded_2(currents, ((("box", "dir"), 0),), near_reach)
    local_near = near_list - (lax.axis_index(("box", "dir")) * leaf_dev - near_reach)
    near_rows = padded[local_near].reshape(leaf_dev, -1)
    stacked = near_matrix.reshape(-1, near_matrix.shape[2])
    return fields + jnp.dot(near_rows, stacked, preferred_element_type=jnp.float32)


def solution(mesh):
    placed = (
        P(("box", "dir"), None),
        P(("box", "dir"), None),
        P(),
        P(),
        P(),
        P(),
        P(),
        P(),
        P(None, None, "dir"),
        P(),
    )
    return jax.shard_map(
        on_device, mesh=mesh, in_specs=placed, out_specs=P(("box", "dir"), None), check_vma=False
    )
```

profile of v0, /device:TPU:0, one launch (start us, length us, event | category | flops | bytes accessed | tf_op | source)
XLA Modules:
  0.0 144.3 jit_solution(13922357546368831117)
XLA Ops:
  1.3 5.2 %fusion.2 = f32[64,4096]{1,0:T(8,128)S(1)} fusion(bf16[1024,4096]{1,0:T(8,128)(2,1)} %param.15, bf16[64,512]{1,0:T(8,128)(2,1)} %param.10, bf16[512,1024]{1,0:T(8,128)(2,1)S(1)} %copy-done), kind=kOutput, calls=%fused_computation.45 | convolution fusion | flops 604045312 | bytes 10551296 | tf_op jit(solution)/shard_map/dot_general | solution.py:48
  7.7 1.7 %reshape.367 = bf16[8,2,2048]{2,1,0:T(2,128)(2,1)} reshape(bf16[2048,2,8]{2,1,0:T(2,128)(2,1)S(1)} %bitcast.135) | data formatting | bytes 131072
  9.4 6.4 %all-to-all-start = ((bf16[8,2,2048]{2,1,0:T(2,128)(2,1)}), bf16[8,2,2048]{2,1,0:T(2,128)(2,1)S(1)}, u32[]{:S(2)}, u32[]{:S(2)}) async-start(bf16[8,2,2048]{2,1,0:T(2,128)(2,1)} %reshape.367), calls=%async_computation | async-start | bytes 131072 | tf_op jit(solution)/shard_map/all_to_all | solution.py:56
  15.8 2.4 %collective-permute-start.2 = (bf16[32,512]{1,0:T(8,128)(2,1)S(1)}, bf16[32,512]{1,0:T(8,128)(2,1)S(1)}, u32[]{:S(2)}, u32[]{:S(2)}) collective-permute-start(bf16[32,512]{1,0:T(8,128)(2,1)S(1)} %get-tuple-element.15), channel_id=1, source_target_pairs={{0,1},{1,2},{2,3},{3,4},{4,5},{5,6},{6,7},{7,8},{8,9},{9,10},{10,1... | collective-permute-start | bytes 98312 | tf_op jit(solution)/shard_map/ppermute | solution.py:12
  55.7 8.0 %collective-permute-start = (bf16[32,2,256]{2,1,0:T(2,128)(2,1)S(1)}, bf16[32,2,256]{2,1,0:T(2,128)(2,1)S(1)}, u32[]{:S(2)}, u32[]{:S(2)}) collective-permute-start(bf16[32,2,256]{2,1,0:T(2,128)(2,1)S(1)} %bitcast.145), channel_id=1, source_target_pairs={{0,8},{8,16},{16,24},{1,9},{9,17},{17,25},{2,10},{10,18},{18,26},{... | collective-permute-start | bytes 98312 | tf_op jit(solution)/shard_map/ppermute | solution.py:12
  65.3 6.1 %gather_fusion.40 = bf16[1728,512]{1,0:T(8,128)(2,1)} fusion(bf16[128,512]{1,0:T(8,128)(2,1)S(1)} %pad_maximum_fusion, s32[2048]{0:T(1024)S(1)} %pad_clamp_fusion), kind=kCustom, calls=%fused_computation.40 | custom fusion | bytes 3545856 | tf_op jit(solution)/shard_map/gather | solution.py:85
  71.4 2.5 %reshape.357 = bf16[64,27,512]{2,1,0:T(8,128)(2,1)S(1)} reshape(bf16[1728,512]{1,0:T(8,128)(2,1)} %gather_fusion.40) | data formatting | bytes 3538944 | tf_op jit(solution)/shard_map/gather | solution.py:85
  77.0 1.5 %gather_fusion.1 = f32[64,2,256]{2,1,0:T(2,128)} fusion(f32[128,2,256]{2,1,0:T(2,128)S(1)} %maximum_convert_fusion, s32[1024]{0:T(1024)} %get-tuple-element.76), kind=kCustom, calls=%fused_computation.1 | custom fusion | bytes 262400 | tf_op jit(solution)/shard_map/gather | solution.py:26
  78.4 1.5 %gather_fusion.11 = f32[64,2,256]{2,1,0:T(2,128)} fusion(f32[128,2,256]{2,1,0:T(2,128)S(1)} %maximum_convert_fusion, s32[1024]{0:T(1024)} %get-tuple-element.73), kind=kCustom, calls=%fused_computation.11 | custom fusion | bytes 262400 | tf_op jit(solution)/shard_map/gather | solution.py:26
  79.9 1.5 %gather_fusion.13 = f32[64,2,256]{2,1,0:T(2,128)} fusion(f32[128,2,256]{2,1,0:T(2,128)S(1)} %maximum_convert_fusion, s32[1024]{0:T(1024)} %get-tuple-element.72), kind=kCustom, calls=%fused_computation.13 | custom fusion | bytes 262400 | tf_op jit(solution)/shard_map/gather | solution.py:26
  82.9 1.5 %gather_fusion.17 = f32[64,2,256]{2,1,0:T(2,128)} fusion(f32[128,2,256]{2,1,0:T(2,128)S(1)} %maximum_convert_fusion, s32[1024]{0:T(1024)} %get-tuple-element.70), kind=kCustom, calls=%fused_computation.17 | custom fusion | bytes 262400 | tf_op jit(solution)/shard_map/gather | solution.py:26
  84.4 1.5 %gather_fusion.19 = f32[64,2,256]{2,1,0:T(2,128)} fusion(f32[128,2,256]{2,1,0:T(2,128)S(1)} %maximum_convert_fusion, s32[1024]{0:T(1024)} %get-tuple-element.69), kind=kCustom, calls=%fused_computation.19 | custom fusion | bytes 262400 | tf_op jit(solution)/shard_map/gather | solution.py:26
  85.9 1.5 %gather_fusion.21 = f32[64,2,256]{2,1,0:T(2,128)} fusion(f32[128,2,256]{2,1,0:T(2,128)S(1)} %maximum_convert_fusion, s32[1024]{0:T(1024)} %get-tuple-element.68), kind=kCustom, calls=%fused_computation.21 | custom fusion | bytes 262400 | tf_op jit(solution)/shard_map/gather | solution.py:26
  88.8 1.5 %gather_fusion.25 = f32[64,2,256]{2,1,0:T(2,128)} fusion(f32[128,2,256]{2,1,0:T(2,128)S(1)} %maximum_convert_fusion, s32[1024]{0:T(1024)} %get-tuple-element.66), kind=kCustom, calls=%fused_computation.25 | custom fusion | bytes 262400 | tf_op jit(solution)/shard_map/gather | solution.py:26
  91.8 1.5 %gather_fusion.29 = f32[64,2,256]{2,1,0:T(2,128)} fusion(f32[128,2,256]{2,1,0:T(2,128)S(1)} %maximum_convert_fusion, s32[1024]{0:T(1024)} %get-tuple-element.64), kind=kCustom, calls=%fused_computation.29 | custom fusion | bytes 262400 | tf_op jit(solution)/shard_map/gather | solution.py:26
  93.3 1.5 %gather_fusion.31 = f32[64,2,256]{2,1,0:T(2,128)} fusion(f32[128,2,256]{2,1,0:T(2,128)S(1)} %maximum_convert_fusion, s32[1024]{0:T(1024)} %get-tuple-element.63), kind=kCustom, calls=%fused_computation.31 | custom fusion | bytes 262400 | tf_op jit(solution)/shard_map/gather | solution.py:26
  96.2 1.5 %gather_fusion.35 = f32[64,2,256]{2,1,0:T(2,128)} fusion(f32[128,2,256]{2,1,0:T(2,128)S(1)} %maximum_convert_fusion, s32[1024]{0:T(1024)} %get-tuple-element.61), kind=kCustom, calls=%fused_computation.35 | custom fusion | bytes 262400 | tf_op jit(solution)/shard_map/gather | solution.py:26
  97.7 1.5 %gather_fusion.37 = f32[64,2,256]{2,1,0:T(2,128)} fusion(f32[128,2,256]{2,1,0:T(2,128)S(1)} %maximum_convert_fusion, s32[1024]{0:T(1024)} %get-tuple-element.60), kind=kCustom, calls=%fused_computation.37 | custom fusion | bytes 262400 | tf_op jit(solution)/shard_map/gather | solution.py:26
  101.9 1.5 %gather_fusion.39 = f32[64,2,256]{2,1,0:T(2,128)} fusion(f32[128,2,256]{2,1,0:T(2,128)S(1)} %maximum_convert_fusion, s32[1024]{0:T(1024)} %get-tuple-element.59), kind=kCustom, calls=%fused_computation.39 | custom fusion | bytes 262400 | tf_op jit(solution)/shard_map/gather | solution.py:26
  106.1 8.1 %subtract_convert_fusion.1 = bf16[64,1,256]{2,1,0:T(2,128)(2,1)S(1)} fusion(f32[64,2,256]{2,1,0:T(2,128)} %gather_fusion.39, f32[64,2,256]{2,1,0:T(2,128)} %gather_fusion.38, f32[64,2,256]{2,1,0:T(2,128)} %gather_fusion.37, f32[64,2,256]{2,1,0:T(2,128)} %gather_fusion.36, f32[64,2,256]{2,1,0:T(2,128)} %gather_fusion.35, f32[64,2,256]{2,1,0:T(2,128)} %gather_fusion.34, ...), kind=kLoop, calls=%fused_computation.63 | loop fusion | flops 1310720 | bytes 5275648 | tf_op jit(solution)/shard_map/convert.5
  114.2 8.0 %add_convert_fusion.1 = bf16[64,1,256]{2,1,0:T(2,128)(2,1)S(1)} fusion(f32[64,2,256]{2,1,0:T(2,128)} %gather_fusion.39, f32[64,2,256]{2,1,0:T(2,128)} %gather_fusion.38, f32[64,2,256]{2,1,0:T(2,128)} %gather_fusion.37, f32[64,2,256]{2,1,0:T(2,128)} %gather_fusion.36, f32[64,2,256]{2,1,0:T(2,128)} %gather_fusion.35, f32[64,2,256]{2,1,0:T(2,128)} %gather_fusion.34, ...), kind=kLoop, calls=%fused_computation.62 | loop fusion | flops 1310720 | bytes 5275648 | tf_op jit(solution)/shard_map/convert.6
  122.9 3.6 %all-to-all-start.1 = ((bf16[64,2,256]{2,1,0:T(2,128)(2,1)}), bf16[64,2,256]{2,1,0:T(2,128)(2,1)S(1)}, u32[]{:S(2)}, u32[]{:S(2)}) async-start(bf16[64,2,256]{2,1,0:T(2,128)(2,1)} %pad_maximum_fusion.2), calls=%async_computation.1 | async-start | bytes 131072 | tf_op jit(solution)/shard_map/all_to_all | solution.py:68
  126.5 8.0 %fusion.3 = f32[64,512]{1,0:T(8,128)S(1)} fusion(bf16[27,512,512]{2,1,0:T(8,128)(2,1)} %param.19, bf16[64,27,512]{2,1,0:T(8,128)(2,1)S(1)} %reshape.357), kind=kOutput, calls=%fused_computation.47 | convolution fusion | flops 905969664 | bytes 16056320 | tf_op jit(solution)/shard_map/dot_general | solution.py:87
  137.2 7.1 %convolution_add_fusion = f32[64,512]{1,0:T(8,128)} fusion(f32[64,512]{1,0:T(8,128)S(1)} %fusion.3, bf16[1024,512]{1,0:T(8,128)(2,1)} %param.16, bf16[64,4096]{1,0:T(8,128)(2,1)S(1)} %bitcast.137, bf16[1024,4096]{1,0:T(8,128)(2,1)} %param.15), kind=kOutput, calls=%fused_computation.46 | convolution fusion | flops 604078080 | bytes 10223616 | tf_op jit(solution)/shard_map/dot_general | solution.py:81
  (111 shorter events, 58.9 us)
Async XLA Ops:
  0.0 1.3 copy-start
  0.0 15.7 %copy-start.2 = (bf16[64,512]{1,0:T(8,128)(2,1)S(1)}, bf16[64,512]{1,0:T(8,128)(2,1)}, u32[]{:S(2)}) copy-start(bf16[64,512]{1,0:T(8,128)(2,1)} %param.10) | copy-start | bytes 196612
  0.0 19.5 %copy-start.11 = (s32[256,20]{0,1:T(8,128)S(1)}, s32[256,20]{0,1:T(8,128)}, u32[]{:S(2)}) copy-start(s32[256,20]{0,1:T(8,128)} %param.12) | copy-start | bytes 61444
  0.0 20.5 %copy-start.10 = (s32[64,27]{0,1:T(8,128)S(1)}, s32[64,27]{0,1:T(8,128)}, u32[]{:S(2)}) copy-start(s32[64,27]{0,1:T(8,128)} %param.11) | copy-start | bytes 20740
  0.0 26.8 %copy-start.1 = (f32[316,2,256]{2,1,0:T(2,128)S(1)}, f32[316,2,256]{2,1,0:T(2,128)}, u32[]{:S(2)}) copy-start(f32[316,2,256]{2,1,0:T(2,128)} %param.18) | copy-start | bytes 1941508
  1.3 34.4 %copy-start.3 = (f32[8,2048]{1,0:T(8,128)}, f32[8,2048]{1,0:T(8,128)S(1)}, u32[]{:S(2)}) copy-start(f32[8,2048]{1,0:T(8,128)S(1)} %get-tuple-element.13) | copy-start | bytes 196612
  1.3 34.4 %copy-start.5 = (f32[8,2048]{1,0:T(8,128)}, f32[8,2048]{1,0:T(8,128)S(1)}, u32[]{:S(2)}) copy-start(f32[8,2048]{1,0:T(8,128)S(1)} %get-tuple-element.14) | copy-start | bytes 196612
  9.4 44.5 %all-to-all-start = ((bf16[8,2,2048]{2,1,0:T(2,128)(2,1)}), bf16[8,2,2048]{2,1,0:T(2,128)(2,1)S(1)}, u32[]{:S(2)}, u32[]{:S(2)}) async-start(bf16[8,2,2048]{2,1,0:T(2,128)(2,1)} %reshape.367), calls=%async_computation | async-start | bytes 131072 | tf_op jit(solution)/shard_map/all_to_all | solution.py:56
  15.8 49.5 %collective-permute-start.2 = (bf16[32,512]{1,0:T(8,128)(2,1)S(1)}, bf16[32,512]{1,0:T(8,128)(2,1)S(1)}, u32[]{:S(2)}, u32[]{:S(2)}) collective-permute-start(bf16[32,512]{1,0:T(8,128)(2,1)S(1)} %get-tuple-element.15), channel_id=1, source_target_pairs={{0,1},{1,2},{2,3},{3,4},{4,5},{5,6},{6,7},{7,8},{8,9},{9,10},{10,1... | collective-permute-start | bytes 98312 | tf_op jit(solution)/shard_map/ppermute | solution.py:12
  18.2 47.1 %collective-permute-start.3 = (bf16[32,512]{1,0:T(8,128)(2,1)S(1)}, bf16[32,512]{1,0:T(8,128)(2,1)S(1)}, u32[]{:S(2)}, u32[]{:S(2)}) collective-permute-start(bf16[32,512]{1,0:T(8,128)(2,1)S(1)} %get-tuple-element.16), channel_id=1, source_target_pairs={{1,0},{2,1},{3,2},{4,3},{5,4},{6,5},{7,6},{8,7},{9,8},{10,9},{11,1... | collective-permute-start | bytes 98312 | tf_op jit(solution)/shard_map/ppermute | solution.py:15
  55.6 9.6 %copy-start.7 = (bf16[8,2,8,256]{3,2,0,1:T(8,128)(2,1)}, bf16[8,2,8,256]{3,2,0,1:T(8,128)(2,1)S(1)}, u32[]{:S(2)}) copy-start(bf16[8,2,8,256]{3,2,0,1:T(8,128)(2,1)S(1)} %copy.41) | copy-start | bytes 196612
  55.7 19.1 %collective-permute-start = (bf16[32,2,256]{2,1,0:T(2,128)(2,1)S(1)}, bf16[32,2,256]{2,1,0:T(2,128)(2,1)S(1)}, u32[]{:S(2)}, u32[]{:S(2)}) collective-permute-start(bf16[32,2,256]{2,1,0:T(2,128)(2,1)S(1)} %bitcast.145), channel_id=1, source_target_pairs={{0,8},{8,16},{16,24},{1,9},{9,17},{17,25},{2,10},{10,18},{18,26},{... | collective-permute-start | bytes 98312 | tf_op jit(solution)/shard_map/ppermute | solution.py:12
  63.7 11.1 %collective-permute-start.1 = (bf16[32,2,256]{2,1,0:T(2,128)(2,1)S(1)}, bf16[32,2,256]{2,1,0:T(2,128)(2,1)S(1)}, u32[]{:S(2)}, u32[]{:S(2)}) collective-permute-start(bf16[32,2,256]{2,1,0:T(2,128)(2,1)S(1)} %bitcast.146), channel_id=1, source_target_pairs={{8,0},{16,8},{24,16},{9,1},{17,9},{25,17},{10,2},{18,10},{26,18},{... | collective-permute-start | bytes 98312 | tf_op jit(solution)/shard_map/ppermute | solution.py:15
  74.8 0.6 copy-start.8
  75.4 0.6 copy-start.9
  122.9 11.6 %all-to-all-start.1 = ((bf16[64,2,256]{2,1,0:T(2,128)(2,1)}), bf16[64,2,256]{2,1,0:T(2,128)(2,1)S(1)}, u32[]{:S(2)}, u32[]{:S(2)}) async-start(bf16[64,2,256]{2,1,0:T(2,128)(2,1)} %pad_maximum_fusion.2), calls=%async_computation.1 | async-start | bytes 131072 | tf_op jit(solution)/shard_map/all_to_all | solution.py:68
  126.5 8.2 %copy-start.4 = (f32[8,2048]{1,0:T(8,128)S(1)}, f32[8,2048]{1,0:T(8,128)}, u32[]{:S(2)}) copy-start(f32[8,2048]{1,0:T(8,128)} %copy-done.3) | copy-start | bytes 196612
  126.5 8.2 %copy-start.6 = (f32[8,2048]{1,0:T(8,128)S(1)}, f32[8,2048]{1,0:T(8,128)}, u32[]{:S(2)}) copy-start(f32[8,2048]{1,0:T(8,128)} %copy-done.5) | copy-start | bytes 196612
where the time goes:
time: 147 us; the launch traced here: 144 us
  local copies, waits for them, and re-layouts  72.3 us (49%)
  other arithmetic  27.9 us (19%)
  starting transfers between devices  23.1 us (16%)
  matrix products  20.4 us (14%)
    gather x20, local copies, waits for them, and re-layouts, translate(): source_field[row_index[:, slot]]  29.1 us
    gather x20, local copies, waits for them, and re-layouts, translate(): operator = translation[kind_rows[:, slot]]  26.4 us
    another operation x3, other arithmetic  17.1 us
    ppermute x2, starting transfers between devices, padded_2(): lax.ppermute(lax.slice_in_dim(block, block.shape[dim] - width, None, axis...  10.4 us
    gather x2, local copies, waits for them, and re-layouts, on_device(): near_rows = padded[local_near].reshape(leaf_dev, -1)  8.59 us
    dot_general x1, matrix products, on_device(): jnp.dot(near_rows, stacked, preferred_element_type=jnp.float32)  8.04 us
    dot_general x1, matrix products, on_device(): fields = jnp.dot(back_pattern, receive, preferred_element_type=jnp.float32)  7.14 us
    all_to_all x1, starting transfers between devices, on_device(): lax.all_to_all(parent.astype(jnp.bfloat16), 'dir', split_axis=2, concat_a...  6.36 us
  transfers between devices with their start and end apart: 6, of which 0 were waited for; matrix products, arithmetic and copies ran while one was open for 37% of the time, Pallas kernels for 0%

commit v1 on v0

v1 whole, which is shorter than its diff:
```python
import functools

import jax
import jax.numpy as jnp
from jax import lax
from jax.experimental import pallas as pl
from jax.experimental.pallas import tpu as pltpu
from jax.sharding import PartitionSpec as P

MESH = pl.DeviceIdType.MESH
LANES = 128
F32 = jnp.float32
BF16 = jnp.bfloat16


def kernel(
    boxes,
    dirs,
    far_ref,
    kind_ref,
    currents,
    near_list,
    shift_angle,
    aggregate,
    interp,
    receive,
    translation,
    near_matrix,
    out,
    agg_vm,
    interp_vm,
    receive_vm,
    trans_vm,
    near_vm,
    padded,
    near_index,
    cosine,
    sine_part,
    pattern,
    send_up,
    upper,
    operator,
    source,
    local,
    send_back,
    returned,
    near_acc,
    back_acc,
    misc_sem,
    interp_sem,
    near_sem,
    halo_send,
    halo_recv,
    up_send,
    up_recv,
    back_send,
    back_recv,
):
    box = lax.axis_index("box")
    me = lax.axis_index("dir")
    leaf_dev, cur = currents.shape
    own = leaf_dev // 8
    reach = leaf_dev // 2
    half = dirs // 2
    slots, _, _ = near_matrix.shape
    directions = shift_angle.shape[1]
    width = directions // dirs
    chunks = width // LANES
    far = far_ref.shape[1]

    def slice_of(step):
        return lax.rem(me + 1 + step, dirs)

    def interp_copies(j):
        for part in range(2):
            yield pltpu.make_async_copy(
                interp.at[:, pl.ds(pl.multiple_of(part * directions + j * width, LANES), width)],
                interp_vm.at[j, :, pl.ds(part * width, width)],
                interp_sem.at[part, j],
            )

    def near_copy(n):
        return pltpu.make_async_copy(near_matrix.at[n], near_vm.at[n], near_sem.at[n])

    agg_copy = pltpu.make_async_copy(aggregate, agg_vm, misc_sem.at[0])
    receive_copy = pltpu.make_async_copy(receive, receive_vm, misc_sem.at[1])
    trans_copy = pltpu.make_async_copy(translation, trans_vm, misc_sem.at[2])
    own_copy = pltpu.make_async_copy(currents, padded.at[pl.ds(reach, leaf_dev)], misc_sem.at[3])
    agg_copy.start()
    own_copy.start()

    @pl.loop(0, dirs)
    def _(step):
        for copy in interp_copies(slice_of(step)):
            copy.start()

    trans_copy.start()

    @pl.loop(0, slots)
    def _(n):
        near_copy(n).start()

    receive_copy.start()

    below = lax.rem(box + boxes - 1, boxes)
    above = lax.rem(box + 1, boxes)
    other = jnp.where(me < half, below, above)
    barrier = pltpu.get_barrier_semaphore()

    @pl.loop(1, dirs)
    def _(k):
        pl.semaphore_signal(
            barrier, inc=1, device_id=(box, lax.rem(me + k, dirs)), device_id_type=MESH
        )

    @pl.loop(0, half)
    def _(k):
        pl.semaphore_signal(barrier, inc=1, device_id=(below, half + k), device_id_type=MESH)
        pl.semaphore_signal(barrier, inc=1, device_id=(above, k), device_id_type=MESH)

    cosine[...] = jnp.cos(shift_angle[...])
    sine_part[...] = jnp.sin(shift_angle[...])
    first_leaf = (box * dirs + me) * leaf_dev - reach
    near_index[...] = (near_list[...] - first_leaf).astype(F32)

    pl.semaphore_wait(barrier, 2 * dirs - 1)

    left = (jnp.where(me == 0, below, box), lax.rem(me + dirs - 1, dirs))
    right = (jnp.where(me == dirs - 1, above, box), lax.rem(me + 1, dirs))
    to_left = pltpu.make_async_remote_copy(
        src_ref=currents.at[pl.ds(0, reach)],
        dst_ref=padded.at[pl.ds(reach + leaf_dev, reach)],
        send_sem=halo_send.at[0],
        recv_sem=halo_recv.at[0],
        device_id=left,
        device_id_type=MESH,
    )
    to_right = pltpu.make_async_remote_copy(
        src_ref=currents.at[pl.ds(leaf_dev - reach, reach)],
        dst_ref=padded.at[pl.ds(0, reach)],
        send_sem=halo_send.at[1],
        recv_sem=halo_recv.at[1],
        device_id=right,
        device_id_type=MESH,
    )
    to_left.start()
    to_right.start()

    agg_copy.wait()
    pattern[...] = jnp.dot(currents[...], agg_vm[...], preferred_element_type=F32).astype(BF16)

    my_slot = half + me
    other_slot = jnp.where(me < half, my_slot + dirs, my_slot - dirs)

    def up_copy(group, j, kind):
        return pltpu.make_async_remote_copy(
            src_ref=send_up.at[j],
            dst_ref=upper.at[(my_slot, other_slot)[kind]],
            send_sem=up_send.at[kind, j],
            recv_sem=up_recv.at[(my_slot, other_slot)[kind]],
            device_id=(group, j),
            device_id_type=MESH,
        )

    def forward(j):
        for copy in interp_copies(j):
            copy.wait()
        children = jnp.dot(pattern[...], interp_vm[j], preferred_element_type=F32)
        lanes = pl.ds(pl.multiple_of(j * width, LANES), width)
        cos, sin = cosine[:, lanes][None], sine_part[:, lanes][None]
        real = children[:, :width].reshape(own, 8, width)
        imag = children[:, width:].reshape(own, 8, width)
        real_part = jnp.sum(real * cos - imag * sin, axis=1)
        imag_part = jnp.sum(real * sin + imag * cos, axis=1)
        pieces = [
            part[:, t * LANES : (t + 1) * LANES]
            for part in (real_part, imag_part)
            for t in range(chunks)
        ]
        return jnp.concatenate(pieces, axis=0).astype(BF16)

    @pl.loop(0, dirs - 1)
    def _(step):
        j = slice_of(step)
        send_up[j] = forward(j)
        up_copy(other, j, 1).start()
        up_copy(box, j, 0).start()

    last = forward(me)
    send_up[me] = last
    up_copy(other, me, 1).start()
    upper[my_slot] = last

    trans_copy.wait()
    for s in range(4 * chunks):
        part, t = s // (2 * chunks), s % chunks
        operator[:, s, :] = trans_vm[:, part, t * LANES : (t + 1) * LANES]

    own_copy.wait()
    to_left.wait_recv()
    to_right.wait_recv()
    near_acc[...] = jnp.zeros_like(near_acc)

    def near_step(n):
        column_of = lax.broadcasted_iota(jnp.int32, near_index.shape, 1)
        column = jnp.sum(
            jnp.where(column_of == n, near_index[...], 0.0), axis=1, keepdims=True
        )
        row_of = lax.broadcasted_iota(jnp.int32, (leaf_dev, 2 * leaf_dev), 1).astype(F32)
        pick = jnp.where(row_of == column, 1.0, 0.0).astype(BF16)
        rows = jnp.dot(pick, padded[...], preferred_element_type=F32).astype(BF16)
        near_copy(n).wait()
        near_acc[...] += jnp.dot(rows, near_vm[n], preferred_element_type=F32)

    early = max(slots - dirs, 0)

    @pl.loop(0, early)
    def _(n):
        near_step(n)

    @pl.loop(1, 2 * dirs)
    def _(k):
        e = lax.rem(my_slot + k, 2 * dirs)
        pltpu.make_async_remote_copy(
            src_ref=upper.at[e],
            dst_ref=upper.at[e],
            send_sem=up_send.at[0, 0],
            recv_sem=up_recv.at[e],
            device_id=(box, me),
            device_id_type=MESH,
        ).wait_recv()

    @pl.loop(0, 2 * dirs)
    def _(e):
        block = upper[e].astype(F32)
        part = [block[own * c : own * (c + 1)] for c in range(2 * chunks)]
        rows = pl.ds(pl.multiple_of(e * own, own), own)
        turned = part + [-x for x in part[chunks:]] + part[:chunks]
        for s in range(4 * chunks):
            source[rows, s, :] = turned[s]

    def back_copy(j):
        return pltpu.make_async_remote_copy(
            src_ref=send_back.at[j],
            dst_ref=returned.at[me],
            send_sem=back_send.at[j],
            recv_sem=back_recv.at[me],
            device_id=(box, j),
            device_id_type=MESH,
        )

    def translate(j):
        @pl.loop(0, own)
        def _(r):
            p = j * own + r
            sums = [None] * 4
            for k in range(far):
                term = operator[kind_ref[p, k]] * source[far_ref[p, k]]
                sums[k % 4] = term if sums[k % 4] is None else sums[k % 4] + term
            total = (sums[0] + sums[1]) + (sums[2] + sums[3])
            local[p] = total[: 2 * chunks] + total[2 * chunks :]

        rows = pl.ds(pl.multiple_of(j * own, own), own)
        return jnp.concatenate([local[rows, c, :] for c in range(2 * chunks)], axis=0).astype(BF16)

    @pl.loop(0, dirs - 1)
    def _(step):
        j = slice_of(step)
        send_back[j] = translate(j)
        back_copy(j).start()

        @pl.when(early + step < slots)
        def _():
            near_step(early + step)

    returned[me] = translate(me)

    @pl.loop(early + dirs - 1, slots)
    def _(n):
        near_step(n)

    back_acc[...] = jnp.zeros_like(back_acc)

    def backward(j):
        block = returned[j].astype(F32)
        part = [block[own * c : own * (c + 1)] for c in range(2 * chunks)]
        real = jnp.concatenate(part[:chunks], axis=1)[:, None]
        imag = jnp.concatenate(part[chunks:], axis=1)[:, None]
        lanes = pl.ds(pl.multiple_of(j * width, LANES), width)
        cos, sin = cosine[:, lanes][None], sine_part[:, lanes][None]
        rot_real = (real * cos + imag * sin).reshape(leaf_dev, width)
        rot_imag = (imag * cos - real * sin).reshape(leaf_dev, width)
        received = jnp.concatenate([rot_real, rot_imag], axis=1).astype(BF16)
        back_acc[...] += lax.dot_general(
            received, interp_vm[j], (((1,), (1,)), ((), ())), preferred_element_type=F32
        )

    backward(me)

    @pl.loop(1, dirs)
    def _(k):
        j = lax.rem(me + dirs - k, dirs)
        pltpu.make_async_remote_copy(
            src_ref=returned.at[j],
            dst_ref=returned.at[j],
            send_sem=back_send.at[0],
            recv_sem=back_recv.at[j],
            device_id=(box, me),
            device_id_type=MESH,
        ).wait_recv()
        backward(j)

    receive_copy.wait()
    fields = jnp.dot(back_acc[...].astype(BF16), receive_vm[...], preferred_element_type=F32)
    out[...] = fields + near_acc[...]

    to_left.wait_send()
    to_right.wait_send()
    up_copy(other, me, 1).wait_send()

    @pl.loop(1, dirs)
    def _(k):
        j = lax.rem(me + k, dirs)
        up_copy(other, j, 1).wait_send()
        up_copy(box, j, 0).wait_send()
        back_copy(j).wait_send()


def on_device(
    boxes,
    dirs,
    currents,
    near_list,
    far_list,
    far_kind,
    aggregate,
    interp,
    receive,
    shift_angle,
    translation,
    near_matrix,
):
    leaf_dev, cur = currents.shape
    patterns = aggregate.shape[1]
    own = leaf_dev // 8
    upper_rows = own * dirs
    directions = shift_angle.shape[1]
    width = directions // dirs
    chunks = width // LANES
    kinds = translation.shape[0]
    slots = near_matrix.shape[0]
    first_row = lax.axis_index("box") * upper_rows
    my_far = lax.dynamic_slice_in_dim(far_list, first_row, upper_rows, 0)
    my_far = my_far - (first_row - upper_rows // 2)
    my_kind = lax.dynamic_slice_in_dim(far_kind, first_row, upper_rows, 0)
    smem = pl.BlockSpec(memory_space=pltpu.SMEM)
    vmem = pl.BlockSpec(memory_space=pltpu.VMEM)
    anywhere = pl.BlockSpec(memory_space=pl.ANY)
    message = (2 * chunks * own, LANES)
    dma = pltpu.SemaphoreType.DMA
    return pl.pallas_call(
        functools.partial(kernel, boxes, dirs),
        out_shape=jax.ShapeDtypeStruct((leaf_dev, receive.shape[1]), F32),
        in_specs=[smem, smem, vmem, vmem, vmem] + [anywhere] * 5,
        out_specs=vmem,
        scratch_shapes=[
            pltpu.VMEM(aggregate.shape, BF16),
            pltpu.VMEM((dirs, patterns, 2 * width), BF16),
            pltpu.VMEM(receive.shape, BF16),
            pltpu.VMEM(translation.shape, F32),
            pltpu.VMEM(near_matrix.shape, BF16),
            pltpu.VMEM((2 * leaf_dev, cur), BF16),
            pltpu.VMEM(near_list.shape, F32),
            pltpu.VMEM(shift_angle.shape, F32),
            pltpu.VMEM(shift_angle.shape, F32),
            pltpu.VMEM((leaf_dev, patterns), BF16),
            pltpu.VMEM((dirs,) + message, BF16),
            pltpu.VMEM((2 * dirs,) + message, BF16),
            pltpu.VMEM((kinds, 4 * chunks, LANES), F32),
            pltpu.VMEM((2 * upper_rows, 4 * chunks, LANES), F32),
            pltpu.VMEM((upper_rows, 2 * chunks, LANES), F32),
            pltpu.VMEM((dirs,) + message, BF16),
            pltpu.VMEM((dirs,) + message, BF16),
            pltpu.VMEM((leaf_dev, cur), F32),
            pltpu.VMEM((leaf_dev, patterns), F32),
            dma((4,)),
            dma((2, dirs)),
            dma((slots,)),
            dma((2,)),
            dma((2,)),
            dma((2, dirs)),
            dma((2 * dirs,)),
            dma((dirs,)),
            dma((dirs,)),
        ],
        compiler_params=pltpu.CompilerParams(
            collective_id=0, has_side_effects=True, vmem_limit_bytes=60 * 1024 * 1024
        ),
    )(
        my_far,
        my_kind,
        currents,
        near_list,
        shift_angle,
        aggregate,
        interp,
        receive,
        translation,
        near_matrix,
    )


def solution(mesh):
    placed = (
        P(("box", "dir"), None),
        P(("box", "dir"), None),
        P(),
        P(),
        P(),
        P(),
        P(),
        P(),
        P(None, None, "dir"),
        P(),
    )
    return jax.shard_map(
        functools.partial(on_device, mesh.shape["box"], mesh.shape["dir"]),
        mesh=mesh,
        in_specs=placed,
        out_specs=P(("box", "dir"), None),
        check_vma=False,
    )
```

time: 147 us -> 40.3 us (0.27); the launches traced: 144 us -> 40 us
  local copies, waits for them, and re-layouts: 72.3 us -> 4.57 us
  Pallas kernels: 0 us -> 34.7 us
  other arithmetic: 27.9 us -> 0.62 us
  starting transfers between devices: 23.1 us -> 0 us
  matrix products: 20.4 us -> 0 us
    gather x42 -> x0, local copies, waits for them, and re-layouts: 64.2 us -> none  [the longest x20 29.1 us: translate(): source_field[row_index[:, slot]]]
    pallas_call x0 -> x1, Pallas kernels: none -> 34.7 us  [on_device(): pl.pallas_call(functools.partial(kernel, boxes, dirs), out_shape=jax.Shap...]
    dot_general x3 -> x0, matrix products: 20.4 us -> none  [the longest x1 8.04 us: on_device(): jnp.dot(near_rows, stacked, preferred_element_type=jnp.float32)]
    another operation x5 -> x0, other arithmetic: 17.9 us -> none
    ppermute x4 -> x0, starting transfers between devices: 13.1 us -> none  [the longest x2 10.4 us: padded_2(): lax.ppermute(lax.slice_in_dim(block, block.shape[dim] - width, None, axis...]
    all_to_all x2 -> x0, starting transfers between devices: 9.93 us -> none  [the longest x1 6.36 us: on_device(): lax.all_to_all(parent.astype(jnp.bfloat16), 'dir', split_axis=2, concat_a...]
    gather x24 -> x0, other arithmetic: 5.49 us -> none  [the longest x11 5.41 us: translate(): source_field[row_index[:, slot]]]
    select_n x4 -> x0, other arithmetic: 1.95 us -> none  [the longest x2 1.93 us: translate(): operator = translation[kind_rows[:, slot]]]
  transfers between devices with their start and end apart: 6 -> 0, of which waited for: 0 -> 0; matrix products, arithmetic and copies ran while one was open for 37% -> 0% of each run, Pallas kernels for 0% -> 0%
where the time goes in v1:
time: 40.3 us; the launch traced here: 40 us
  Pallas kernels  34.7 us (86%)
  local copies, waits for them, and re-layouts  4.57 us (11%)
  other arithmetic  0.62 us (2%)
    pallas_call x1, Pallas kernels, on_device(): pl.pallas_call(functools.partial(kernel, boxes, dirs), out_shape=jax.Shap...  34.7 us
    unnamed x4, local copies, waits for them, and re-layouts  3.78 us

profile of v1, /device:TPU:0, one launch (start us, length us, event | category | flops | bytes accessed | tf_op | source)
XLA Modules:
  0.0 40.0 jit_solution(5743391063356881297)
XLA Ops:
  0.0 0.8 %constant_dynamic-slice_fusion = (s32[64,20]{0,1:T(8,128)S(1)}, s32[64,20]{0,1:T(8,128)S(1)}) fusion(s32[256,20]{0,1:T(8,128)} %param.13, s32[]{:T(128)S(6)} %select_n.4, s32[256,20]{0,1:T(8,128)} %param.12), kind=kLoop, calls=%fused_computation.1 | loop fusion | bytes 20484 | tf_op jit(solution)/shard_map/dynamic_slice | solution.py:355
  0.8 0.7 %copy.15.kind_ref = s32[64,20]{1,0:T(8,128)} copy(s32[64,20]{0,1:T(8,128)S(1)} %get-tuple-element.5) | data formatting | bytes 10240
  1.5 0.1 copy.14
  1.6 0.6 %broadcast_subtract_fusion.far_ref = s32[64,20]{1,0:T(8,128)} fusion(s32[64,20]{1,0:T(8,128)S(1)} %copy.14, s32[]{:T(128)S(6)} %sub.9), kind=kLoop, calls=%fused_computation | loop fusion | flops 1280 | bytes 10244 | tf_op jit(solution)/shard_map/sub | solution.py:354
  2.2 1.4 %copy.13.near_list = s32[64,27]{1,0:T(8,128)} copy(s32[64,27]{0,1:T(8,128)} %param.11) | data formatting | bytes 13824 | tf_op args[1]
  3.6 34.7 %shard_map.100 = f32[64,512]{1,0:T(8,128)} custom-call(s32[64,20]{1,0:T(8,128)} %broadcast_subtract_fusion.far_ref, s32[64,20]{1,0:T(8,128)} %copy.15.kind_ref, bf16[64,512]{1,0:T(8,128)(2,1)} %currents.1, s32[64,27]{1,0:T(8,128)} %copy.13.near_list, f32[8,2048]{1,0:T(8,128)} %shift_angle.1, bf16[512,1024]{1,0:T(8,128)(2,1)} %aggregate.1, ...), custom_call_target="tpu_custom_call" | custom-call | tf_op jit(solution)/shard_map/pallas_call | solution.py:361
  38.4 1.6 %copy.17 = f32[64,512]{1,0:T(8,128)} copy(f32[64,512]{1,0:T(8,128)} %shard_map.100) | data formatting | bytes 262144

commit v2 on v1

--- a/solution.py
+++ b/solution.py
@@ -16,8 +16,8 @@
 def kernel(
     boxes,
     dirs,
-    far_ref,
-    kind_ref,
+    far_list,
+    far_kind,
     currents,
     near_list,
     shift_angle,
@@ -32,8 +32,10 @@
     receive_vm,
     trans_vm,
     near_vm,
+    far_ref,
+    kind_ref,
     padded,
-    near_index,
+    near_rows,
     cosine,
     sine_part,
     pattern,
@@ -62,11 +64,13 @@
     own = leaf_dev // 8
     reach = leaf_dev // 2
     half = dirs // 2
-    slots, _, _ = near_matrix.shape
+    slots = near_list.shape[0]
+    groups, depth = near_vm.shape[:2]
+    batch = slots // groups
     directions = shift_angle.shape[1]
     width = directions // dirs
     chunks = width // LANES
-    far = far_ref.shape[1]
+    far = far_ref.shape[0]
 
     def slice_of(step):
         return lax.rem(me + 1 + step, dirs)
@@ -79,26 +83,31 @@
                 interp_sem.at[part, j],
             )
 
-    def near_copy(n):
-        return pltpu.make_async_copy(near_matrix.at[n], near_vm.at[n], near_sem.at[n])
+    def near_copy(g):
+        rows = pl.ds(pl.multiple_of(g * depth, depth), depth)
+        return pltpu.make_async_copy(near_matrix.at[rows], near_vm.at[g], near_sem.at[g])
 
     agg_copy = pltpu.make_async_copy(aggregate, agg_vm, misc_sem.at[0])
     receive_copy = pltpu.make_async_copy(receive, receive_vm, misc_sem.at[1])
     trans_copy = pltpu.make_async_copy(translation, trans_vm, misc_sem.at[2])
     own_copy = pltpu.make_async_copy(currents, padded.at[pl.ds(reach, leaf_dev)], misc_sem.at[3])
+    far_copy = pltpu.make_async_copy(far_list, far_ref, misc_sem.at[4])
+    kind_copy = pltpu.make_async_copy(far_kind, kind_ref, misc_sem.at[5])
     agg_copy.start()
     own_copy.start()
+    trans_copy.start()
 
     @pl.loop(0, dirs)
     def _(step):
         for copy in interp_copies(slice_of(step)):
             copy.start()
 
-    trans_copy.start()
-
-    @pl.loop(0, slots)
-    def _(n):
-        near_copy(n).start()
+    far_copy.start()
+    kind_copy.start()
+
+    @pl.loop(0, groups)
+    def _(g):
+        near_copy(g).start()
 
     receive_copy.start()
 
@@ -120,8 +129,9 @@
 
     cosine[...] = jnp.cos(shift_angle[...])
     sine_part[...] = jnp.sin(shift_angle[...])
-    first_leaf = (box * dirs + me) * leaf_dev - reach
-    near_index[...] = (near_list[...] - first_leaf).astype(F32)
+
+    agg_copy.wait()
+    pattern[...] = jnp.dot(currents[...], agg_vm[...], preferred_element_type=F32).astype(BF16)
 
     pl.semaphore_wait(barrier, 2 * dirs - 1)
 
@@ -146,8 +156,10 @@
     to_left.start()
     to_right.start()
 
-    agg_copy.wait()
-    pattern[...] = jnp.dot(currents[...], agg_vm[...], preferred_element_type=F32).astype(BF16)
+    trans_copy.wait()
+    for s in range(4 * chunks):
+        part, t = s // (2 * chunks), s % chunks
+        operator[:, s, :] = trans_vm[:, part, t * LANES : (t + 1) * LANES]
 
     my_slot = half + me
     other_slot = jnp.where(me < half, my_slot + dirs, my_slot - dirs)
@@ -163,8 +175,6 @@
         )
 
     def forward(j):
-        for copy in interp_copies(j):
-            copy.wait()
         children = jnp.dot(pattern[...], interp_vm[j], preferred_element_type=F32)
         lanes = pl.ds(pl.multiple_of(j * width, LANES), width)
         cos, sin = cosine[:, lanes][None], sine_part[:, lanes][None]
@@ -179,44 +189,51 @@
         ]
         return jnp.concatenate(pieces, axis=0).astype(BF16)
 
-    @pl.loop(0, dirs - 1)
+    def forward_pair(first, second):
+        for j in (first, second):
+            for copy in interp_copies(j):
+                copy.wait()
+        one, two = forward(first), forward(second)
+        send_up[first] = one
+        send_up[second] = two
+        up_copy(other, first, 1).start()
+        up_copy(box, first, 0).start()
+        up_copy(other, second, 1).start()
+        return two
+
+    @pl.loop(0, dirs // 2 - 1)
     def _(step):
-        j = slice_of(step)
-        send_up[j] = forward(j)
-        up_copy(other, j, 1).start()
-        up_copy(box, j, 0).start()
-
-    last = forward(me)
-    send_up[me] = last
-    up_copy(other, me, 1).start()
-    upper[my_slot] = last
-
-    trans_copy.wait()
-    for s in range(4 * chunks):
-        part, t = s // (2 * chunks), s % chunks
-        operator[:, s, :] = trans_vm[:, part, t * LANES : (t + 1) * LANES]
+        second = slice_of(2 * step + 1)
+        forward_pair(slice_of(2 * step), second)
+        up_copy(box, second, 0).start()
+
+    upper[my_slot] = forward_pair(slice_of(dirs - 2), me)
 
     own_copy.wait()
     to_left.wait_recv()
     to_right.wait_recv()
+    first_leaf = (box * dirs + me) * leaf_dev - reach
+    index = (near_list[...] - first_leaf).astype(F32).T
+    row_of = lax.broadcasted_iota(jnp.int32, (leaf_dev, 2 * leaf_dev), 1).astype(F32)
+    for n in range(slots):
+        pick = jnp.where(row_of == index[:, n : n + 1], 1.0, 0.0).astype(BF16)
+        rows = jnp.dot(pick, padded[...], preferred_element_type=F32).astype(BF16)
+        near_rows[n // batch, :, (n % batch) * cur : (n % batch + 1) * cur] = rows
+
     near_acc[...] = jnp.zeros_like(near_acc)
 
-    def near_step(n):
-        column_of = lax.broadcasted_iota(jnp.int32, near_index.shape, 1)
-        column = jnp.sum(
-            jnp.where(column_of == n, near_index[...], 0.0), axis=1, keepdims=True
-        )
-        row_of = lax.broadcasted_iota(jnp.int32, (leaf_dev, 2 * leaf_dev), 1).astype(F32)
-        pick = jnp.where(row_of == column, 1.0, 0.0).astype(BF16)
-        rows = jnp.dot(pick, padded[...], preferred_element_type=F32).astype(BF16)
-        near_copy(n).wait()
-        near_acc[...] += jnp.dot(rows, near_vm[n], preferred_element_type=F32)
-
-    early = max(slots - dirs, 0)
+    def near_group(g):
+        near_copy(g).wait()
+        near_acc[...] += jnp.dot(near_rows[g], near_vm[g], preferred_element_type=F32)
+
+    early = (groups + 1) // 2
 
     @pl.loop(0, early)
-    def _(n):
-        near_step(n)
+    def _(g):
+        near_group(g)
+
+    far_copy.wait()
+    kind_copy.wait()
 
     @pl.loop(1, 2 * dirs)
     def _(k):
@@ -230,14 +247,19 @@
             device_id_type=MESH,
         ).wait_recv()
 
-    @pl.loop(0, 2 * dirs)
-    def _(e):
+    def spread(e):
         block = upper[e].astype(F32)
         part = [block[own * c : own * (c + 1)] for c in range(2 * chunks)]
-        rows = pl.ds(pl.multiple_of(e * own, own), own)
+        place = lax.rem(e + box * dirs + 2 * dirs - half, 2 * dirs)
+        rows = pl.ds(pl.multiple_of(place * own, own), own)
         turned = part + [-x for x in part[chunks:]] + part[:chunks]
         for s in range(4 * chunks):
             source[rows, s, :] = turned[s]
+
+    @pl.loop(0, dirs // 2)
+    def _(quarter):
+        for k in range(4):
+            spread(4 * quarter + k)
 
     def back_copy(j):
         return pltpu.make_async_remote_copy(
@@ -249,15 +271,22 @@
             device_id_type=MESH,
         )
 
+    first_row = box * dirs * own
+    window = 2 * dirs * own
+
+    def in_window(row):
+        return row & (window - 1) if window & (window - 1) == 0 else lax.rem(row, window)
+
     def translate(j):
-        @pl.loop(0, own)
-        def _(r):
+        for r in range(own):
             p = j * own + r
-            sums = [None] * 4
+            sums = [None] * 2
             for k in range(far):
-                term = operator[kind_ref[p, k]] * source[far_ref[p, k]]
-                sums[k % 4] = term if sums[k % 4] is None else sums[k % 4] + term
-            total = (sums[0] + sums[1]) + (sums[2] + sums[3])
+                kind = kind_ref[k, first_row + p]
+                row = in_window(far_ref[k, first_row + p])
+                term = operator[kind] * source[row]
+                sums[k % 2] = term if sums[k % 2] is None else sums[k % 2] + term
+            total = sums[0] + sums[1]
             local[p] = total[: 2 * chunks] + total[2 * chunks :]
 
         rows = pl.ds(pl.multiple_of(j * own, own), own)
@@ -269,19 +298,15 @@
         send_back[j] = translate(j)
         back_copy(j).start()
 
-        @pl.when(early + step < slots)
-        def _():
-            near_step(early + step)
-
     returned[me] = translate(me)
 
-    @pl.loop(early + dirs - 1, slots)
-    def _(n):
-        near_step(n)
+    @pl.loop(early, groups)
+    def _(g):
+        near_group(g)
 
     back_acc[...] = jnp.zeros_like(back_acc)
 
-    def backward(j):
+    def received(j):
         block = returned[j].astype(F32)
         part = [block[own * c : own * (c + 1)] for c in range(2 * chunks)]
         real = jnp.concatenate(part[:chunks], axis=1)[:, None]
@@ -290,16 +315,9 @@
         cos, sin = cosine[:, lanes][None], sine_part[:, lanes][None]
         rot_real = (real * cos + imag * sin).reshape(leaf_dev, width)
         rot_imag = (imag * cos - real * sin).reshape(leaf_dev, width)
-        received = jnp.concatenate([rot_real, rot_imag], axis=1).astype(BF16)
-        back_acc[...] += lax.dot_general(
-            received, interp_vm[j], (((1,), (1,)), ((), ())), preferred_element_type=F32
-        )
-
-    backward(me)
-
-    @pl.loop(1, dirs)
-    def _(k):
-        j = lax.rem(me + dirs - k, dirs)
+        return jnp.concatenate([rot_real, rot_imag], axis=1).astype(BF16)
+
+    def back_wait(j):
         pltpu.make_async_remote_copy(
             src_ref=returned.at[j],
             dst_ref=returned.at[j],
@@ -308,7 +326,27 @@
             device_id=(box, me),
             device_id_type=MESH,
         ).wait_recv()
-        backward(j)
+
+    def back_pair(first, second):
+        total = None
+        for j in (first, second):
+            term = lax.dot_general(
+                received(j), interp_vm[j], (((1,), (1,)), ((), ())), preferred_element_type=F32
+            )
+            total = term if total is None else total + term
+        back_acc[...] += total
+
+    nearest = lax.rem(me + dirs - 1, dirs)
+    back_wait(nearest)
+    back_pair(me, nearest)
+
+    @pl.loop(1, dirs // 2)
+    def _(k):
+        first = lax.rem(me + dirs - 2 * k, dirs)
+        second = lax.rem(me + dirs - 2 * k - 1, dirs)
+        back_wait(first)
+        back_wait(second)
+        back_pair(first, second)
 
     receive_copy.wait()
     fields = jnp.dot(back_acc[...].astype(BF16), receive_vm[...], preferred_element_type=F32)
@@ -349,28 +387,27 @@
     chunks = width // LANES
     kinds = translation.shape[0]
     slots = near_matrix.shape[0]
-    first_row = lax.axis_index("box") * upper_rows
-    my_far = lax.dynamic_slice_in_dim(far_list, first_row, upper_rows, 0)
-    my_far = my_far - (first_row - upper_rows // 2)
-    my_kind = lax.dynamic_slice_in_dim(far_kind, first_row, upper_rows, 0)
-    smem = pl.BlockSpec(memory_space=pltpu.SMEM)
+    batch = next(size for size in (3, 2, 1) if slots % size == 0)
+    groups, depth = slots // batch, batch * cur
     vmem = pl.BlockSpec(memory_space=pltpu.VMEM)
-    anywhere = pl.BlockSpec(memory_space=pl.ANY)
+    anywhere = pl.BlockSpec(memory_space=pltpu.HBM)
     message = (2 * chunks * own, LANES)
     dma = pltpu.SemaphoreType.DMA
     return pl.pallas_call(
         functools.partial(kernel, boxes, dirs),
         out_shape=jax.ShapeDtypeStruct((leaf_dev, receive.shape[1]), F32),
-        in_specs=[smem, smem, vmem, vmem, vmem] + [anywhere] * 5,
+        in_specs=[anywhere] * 2 + [vmem] * 3 + [anywhere] * 5,
         out_specs=vmem,
         scratch_shapes=[
             pltpu.VMEM(aggregate.shape, BF16),
             pltpu.VMEM((dirs, patterns, 2 * width), BF16),
             pltpu.VMEM(receive.shape, BF16),
             pltpu.VMEM(translation.shape, F32),
-            pltpu.VMEM(near_matrix.shape, BF16),
+            pltpu.VMEM((groups, depth, near_matrix.shape[2]), BF16),
+            pltpu.SMEM(far_list.shape[::-1], jnp.int32),
+            pltpu.SMEM(far_kind.shape[::-1], jnp.int32),
             pltpu.VMEM((2 * leaf_dev, cur), BF16),
-            pltpu.VMEM(near_list.shape, F32),
+            pltpu.VMEM((groups, leaf_dev, depth), BF16),
             pltpu.VMEM(shift_angle.shape, F32),
             pltpu.VMEM(shift_angle.shape, F32),
             pltpu.VMEM((leaf_dev, patterns), BF16),
@@ -383,9 +420,9 @@
             pltpu.VMEM((dirs,) + message, BF16),
             pltpu.VMEM((leaf_dev, cur), F32),
             pltpu.VMEM((leaf_dev, patterns), F32),
-            dma((4,)),
+            dma((6,)),
             dma((2, dirs)),
-            dma((slots,)),
+            dma((groups,)),
             dma((2,)),
             dma((2,)),
             dma((2, dirs)),
@@ -397,16 +434,16 @@
             collective_id=0, has_side_effects=True, vmem_limit_bytes=60 * 1024 * 1024
         ),
     )(
-        my_far,
-        my_kind,
+        far_list.T,
+        far_kind.T,
         currents,
-        near_list,
+        near_list.T,
         shift_angle,
         aggregate,
         interp,
         receive,
         translation,
-        near_matrix,
+        near_matrix.reshape(-1, near_matrix.shape[2]),
     )
 
 

time: 40.3 us -> 26.4 us (0.66)
  Pallas kernels: 34.7 us -> 24.6 us
  local copies, waits for them, and re-layouts: 4.57 us -> 1.57 us
  other arithmetic: 0.62 us -> 0 us
    pallas_call x1, Pallas kernels: 34.7 us -> 24.6 us  [on_device(): pl.pallas_call(functools.partial(kernel, boxes, dirs), out_shape=jax.Shap...]
    unnamed x4 -> x1, local copies, waits for them, and re-layouts: 3.78 us -> 1.57 us
    dynamic_slice x1 -> x0, local copies, waits for them, and re-layouts: 0.8 us -> none  [on_device(): my_kind = lax.dynamic_slice_in_dim(far_kind, first_row, upper_rows, 0)]
    sub x1 -> x0, other arithmetic: 0.62 us -> none  [on_device(): my_far = my_far - (first_row - upper_rows // 2)]
where the time goes in v2:
time: 26.4 us; the launch traced here: 26.2 us
  Pallas kernels  24.6 us (93%)
  local copies, waits for them, and re-layouts  1.57 us (6%)
    pallas_call x1, Pallas kernels, on_device(): pl.pallas_call(functools.partial(kernel, boxes, dirs), out_shape=jax.Shap...  24.6 us
    unnamed x1, local copies, waits for them, and re-layouts  1.57 us

profile of v2, /device:TPU:0, one launch (start us, length us, event | category | flops | bytes accessed | tf_op | source)
XLA Modules:
  0.0 26.2 jit_solution(17327791815144130323)
XLA Ops:
  0.0 24.6 %shard_map.100 = f32[64,512]{1,0:T(8,128)} custom-call(s32[20,256]{1,0:T(8,128)} %bitcast.5, s32[20,256]{1,0:T(8,128)} %bitcast.6, bf16[64,512]{1,0:T(8,128)(2,1)} %currents.1, s32[27,64]{1,0:T(8,128)} %bitcast.7, f32[8,2048]{1,0:T(8,128)} %shift_angle.1, bf16[512,1024]{1,0:T(8,128)(2,1)} %aggregate.1, bf16[1024,4096]{1,0:T(8,128)(2,1)} %interp.1, ...), custom_call_target="tpu_custom_call" | custom-call | tf_op jit(solution)/shard_map/pallas_call | solution.py:396
  24.6 1.6 %copy.12 = f32[64,512]{1,0:T(8,128)} copy(f32[64,512]{1,0:T(8,128)} %shard_map.100) | data formatting | bytes 262144

commit v3 on v2

--- a/solution.py
+++ b/solution.py
@@ -226,7 +226,7 @@
         near_copy(g).wait()
         near_acc[...] += jnp.dot(near_rows[g], near_vm[g], preferred_element_type=F32)
 
-    early = (groups + 1) // 2
+    early = max(groups - 2, 1)
 
     @pl.loop(0, early)
     def _(g):
@@ -340,8 +340,7 @@
     back_wait(nearest)
     back_pair(me, nearest)
 
-    @pl.loop(1, dirs // 2)
-    def _(k):
+    for k in range(1, dirs // 2):
         first = lax.rem(me + dirs - 2 * k, dirs)
         second = lax.rem(me + dirs - 2 * k - 1, dirs)
         back_wait(first)

time: 26.4 us -> 26 us (0.985)
  Pallas kernels: 24.6 us -> 24.3 us
    pallas_call x1, Pallas kernels: 24.6 us -> 24.3 us  [on_device(): pl.pallas_call(functools.partial(kernel, boxes, dirs), out_shape=jax.Shap...]
where the time goes in v3:
time: 26 us; the launch traced here: 25.9 us
  Pallas kernels  24.3 us (93%)
  local copies, waits for them, and re-layouts  1.57 us (6%)
    pallas_call x1, Pallas kernels, on_device(): pl.pallas_call(functools.partial(kernel, boxes, dirs), out_shape=jax.Shap...  24.3 us
    unnamed x1, local copies, waits for them, and re-layouts  1.57 us

profile of v3, /device:TPU:0, one launch (start us, length us, event | category | flops | bytes accessed | tf_op | source)
XLA Modules:
  0.0 25.9 jit_solution(5525103517230630887)
XLA Ops:
  0.0 24.3 %shard_map.100 = f32[64,512]{1,0:T(8,128)} custom-call(s32[20,256]{1,0:T(8,128)} %bitcast.5, s32[20,256]{1,0:T(8,128)} %bitcast.6, bf16[64,512]{1,0:T(8,128)(2,1)} %currents.1, s32[27,64]{1,0:T(8,128)} %bitcast.7, f32[8,2048]{1,0:T(8,128)} %shift_angle.1, bf16[512,1024]{1,0:T(8,128)(2,1)} %aggregate.1, bf16[1024,4096]{1,0:T(8,128)(2,1)} %interp.1, ...), custom_call_target="tpu_custom_call" | custom-call | tf_op jit(solution)/shard_map/pallas_call | solution.py:395
  24.3 1.6 %copy.12 = f32[64,512]{1,0:T(8,128)} copy(f32[64,512]{1,0:T(8,128)} %shard_map.100) | data formatting | bytes 262144
